TPU v7x, 32 devices: a whole 2x2x4 slice. The times are simulated.
32 devices in a mesh: tm: 8 (over z, y), rep: 4 (over x, core).
Axes of the slice: x: 2, y: 2, z: 4, core: 2. Of those that a mesh axis runs over, the one named last changes fastest.
Arguments:
- transitions: float32 [32, 512, 512], P(('rep', 'tm')), parts along dimension 0, may hold values from -1 to 1, as said below
- cond_covs: float32 [32, 512, 512], P(('rep', 'tm')), parts along dimension 0, may hold values from -40 to 40, as said below
- transition_est: float32 [2048, 512], P('rep'), parts along dimension 0, may hold values from -0.25 to 0.25
Outputs:
- cov_blocks: float32 [32, 512, 512], P(('rep', 'tm')), parts along dimension 0
- transition_grad: float32 [2048, 512], P('rep'), parts along dimension 0
There are 4 independent parts, one for each index of `rep`. A program takes and returns all parts, laid end to end along the dimension named above; each array names one. Nothing has to cross between parts.
Inputs may be any that keep to these rules, and one draw needn't show every extreme that they name: `transitions`: every block has spectral norm below one. `cond_covs`: every block is symmetric and positive definite.
All inputs are finite; a program needn't handle non-finite values.
Results may differ from a plain program's by a relative error of at most 0.00017.
Values sent between devices are 32-bit elements; how exact they have to be, the bound alone decides.
A program may use at most 192 MiB of HBM per device.

v0:
```python
import jax
import jax.numpy as jnp
from jax import lax
from jax.sharding import PartitionSpec as P

highest = lax.Precision.HIGHEST


def passed_along(block, axis, distance):
    devices = range(lax.axis_size(axis))
    route = [(i - distance, i) for i in devices if i - distance in devices]
    return lax.ppermute(block, axis, route)


def times_transposed(left, right):
    return lax.dot_general(
        left, right, (((1,), (1,)), ((), ())), precision=highest, preferred_element_type=jnp.float32
    )


def product(left, right):
    return jnp.dot(left, right, precision=highest, preferred_element_type=jnp.float32)


def on_device(transitions, cond_covs, transition_est):
    blocks_here = transitions.shape[0]
    width = transitions.shape[1]
    devices = lax.axis_size("tm")
    total_blocks = blocks_here * devices
    position = lax.axis_index("tm")
    combined_gain = transitions[blocks_here - 1]
    combined_noise = cond_covs[blocks_here - 1]
    empty_block = jnp.zeros((width, width), jnp.float32)

    def advance(turn_number, incoming):
        outgoing = (
            product(combined_gain, times_transposed(incoming, combined_gain)) + combined_noise
        )
        return passed_along(outgoing, "tm", -1)

    covariance = lax.fori_loop(0, devices - 1, advance, empty_block)
    transition = transitions[0]
    previous_step_cross = times_transposed(covariance, transition)
    covariance = product(transition, previous_step_cross) + cond_covs[0]
    collected = [covariance]
    current_entry = jnp.where(position * blocks_here + 0 < total_blocks - 1, 1.0, 0.0).astype(
        jnp.float32
    )
    accumulated = current_entry * (previous_step_cross - product(transition_est, covariance))
    gradient = lax.psum(accumulated, "tm") / (total_blocks - 1)
    cov_blocks = jnp.stack(collected[::-1], axis=0)
    return (cov_blocks, gradient)


def solution(mesh):
    return jax.shard_map(
        on_device,
        mesh=mesh,
        in_specs=(P(("rep", "tm"), None, None), P(("rep", "tm"), None, None), P("rep", None)),
        out_specs=(P(("rep", "tm"), None, None), P("rep", None)),
        check_vma=False,
    )
```

profile of v0, /device:TPU:0, one launch (start us, length us, event | category | flops | bytes accessed | tf_op | source)
XLA Modules:
  0.0 345.2 jit_solution(12036947720468812156)
XLA Ops:
  7.2 0.0 copy-start
  7.2 0.0 all-reduce.2.cloned.1.call-start
  7.2 2.6 copy.5
  9.8 0.0 copy-start.1
  9.8 0.1 broadcast_in_dim.3
  10.0 1.1 copy-done.1
  11.1 233.2 %while.10 = (s32[]{:T(128)}, f32[512,512]{0,1:T(8,128)S(1)}, f32[512,512]{1,0:T(8,128)S(1)}, f32[512,512]{0,1:T(8,128)}, s32[]{:T(128)}) while((s32[]{:T(128)}, f32[512,512]{0,1:T(8,128)S(1)}, f32[512,512]{1,0:T(8,128)S(1)}, f32[512,512]{0,1:T(8,128)}, s32[]{:T(128)}) %tuple.29), condition=%wide.region_1.0_spmd, body=%wide.region_0.0_spmd.sunk | while | flops 3221487616 | bytes 15728769 | solution.py:41
  11.1 0.0 copy-start.2
  11.1 3.5 %fusion.26 = f32[512,512]{1,0:T(8,128)S(1)} fusion(f32[512,512]{0,1:T(8,128)S(1)} %get-tuple-element.66, f32[512,512]{1,0:T(8,128)S(1)} %get-tuple-element.72), kind=kOutput, calls=%fused_computation.11.clone.1 | convolution fusion | flops 1610612736 | bytes 3145728 | tf_op jit(solution)/shard_map/while/body/eval_jaxpr/dot_general | solution.py:16
  14.5 0.0 copy-done.2
  14.6 4.4 %fusion.27 = f32[512,512]{0,1:T(8,128)} fusion(f32[512,512]{0,1:T(8,128)S(1)} %copy-done.2, f32[512,512]{1,0:T(8,128)S(1)} %fusion.26, f32[512,512]{1,0:T(8,128)S(1)} %get-tuple-element.72), kind=kOutput, calls=%fused_computation.1.clone.1 | convolution fusion | flops 1610874880 | bytes 4194304 | tf_op jit(solution)/shard_map/while/body/eval_jaxpr/dot_general | solution.py:22
  19.0 1.3 collective-permute-start
  20.3 27.0 %collective-permute-done = f32[512,512]{0,1:T(8,128)S(1)} collective-permute-done((f32[512,512]{0,1:T(8,128)}, f32[512,512]{0,1:T(8,128)S(1)}, u32[]{:S(2)}, u32[]{:S(2)}) %collective-permute-start) | collective-permute-done | bytes 1048608 | tf_op jit(solution)/shard_map/while/body/eval_jaxpr/ppermute | solution.py:12
  47.3 0.0 copy-start.2
  47.3 3.5 %fusion.26 = f32[512,512]{1,0:T(8,128)S(1)} fusion(f32[512,512]{0,1:T(8,128)S(1)} %get-tuple-element.66, f32[512,512]{1,0:T(8,128)S(1)} %get-tuple-element.72), kind=kOutput, calls=%fused_computation.11.clone.1 | convolution fusion | flops 1610612736 | bytes 3145728 | tf_op jit(solution)/shard_map/while/body/eval_jaxpr/dot_general | solution.py:16
  50.7 0.0 copy-done.2
  50.7 4.4 %fusion.27 = f32[512,512]{0,1:T(8,128)} fusion(f32[512,512]{0,1:T(8,128)S(1)} %copy-done.2, f32[512,512]{1,0:T(8,128)S(1)} %fusion.26, f32[512,512]{1,0:T(8,128)S(1)} %get-tuple-element.72), kind=kOutput, calls=%fused_computation.1.clone.1 | convolution fusion | flops 1610874880 | bytes 4194304 | tf_op jit(solution)/shard_map/while/body/eval_jaxpr/dot_general | solution.py:22
  55.2 1.3 collective-permute-start
  56.5 25.7 %collective-permute-done = f32[512,512]{0,1:T(8,128)S(1)} collective-permute-done((f32[512,512]{0,1:T(8,128)}, f32[512,512]{0,1:T(8,128)S(1)}, u32[]{:S(2)}, u32[]{:S(2)}) %collective-permute-start) | collective-permute-done | bytes 1048608 | tf_op jit(solution)/shard_map/while/body/eval_jaxpr/ppermute | solution.py:12
  82.2 0.0 copy-start.2
  82.2 3.5 %fusion.26 = f32[512,512]{1,0:T(8,128)S(1)} fusion(f32[512,512]{0,1:T(8,128)S(1)} %get-tuple-element.66, f32[512,512]{1,0:T(8,128)S(1)} %get-tuple-element.72), kind=kOutput, calls=%fused_computation.11.clone.1 | convolution fusion | flops 1610612736 | bytes 3145728 | tf_op jit(solution)/shard_map/while/body/eval_jaxpr/dot_general | solution.py:16
  85.7 0.0 copy-done.2
  85.7 4.4 %fusion.27 = f32[512,512]{0,1:T(8,128)} fusion(f32[512,512]{0,1:T(8,128)S(1)} %copy-done.2, f32[512,512]{1,0:T(8,128)S(1)} %fusion.26, f32[512,512]{1,0:T(8,128)S(1)} %get-tuple-element.72), kind=kOutput, calls=%fused_computation.1.clone.1 | convolution fusion | flops 1610874880 | bytes 4194304 | tf_op jit(solution)/shard_map/while/body/eval_jaxpr/dot_general | solution.py:22
  90.2 1.3 collective-permute-start
  91.5 24.9 %collective-permute-done = f32[512,512]{0,1:T(8,128)S(1)} collective-permute-done((f32[512,512]{0,1:T(8,128)}, f32[512,512]{0,1:T(8,128)S(1)}, u32[]{:S(2)}, u32[]{:S(2)}) %collective-permute-start) | collective-permute-done | bytes 1048608 | tf_op jit(solution)/shard_map/while/body/eval_jaxpr/ppermute | solution.py:12
  116.3 0.0 copy-start.2
  116.3 3.5 %fusion.26 = f32[512,512]{1,0:T(8,128)S(1)} fusion(f32[512,512]{0,1:T(8,128)S(1)} %get-tuple-element.66, f32[512,512]{1,0:T(8,128)S(1)} %get-tuple-element.72), kind=kOutput, calls=%fused_computation.11.clone.1 | convolution fusion | flops 1610612736 | bytes 3145728 | tf_op jit(solution)/shard_map/while/body/eval_jaxpr/dot_general | solution.py:16
  119.8 0.0 copy-done.2
  119.8 4.4 %fusion.27 = f32[512,512]{0,1:T(8,128)} fusion(f32[512,512]{0,1:T(8,128)S(1)} %copy-done.2, f32[512,512]{1,0:T(8,128)S(1)} %fusion.26, f32[512,512]{1,0:T(8,128)S(1)} %get-tuple-element.72), kind=kOutput, calls=%fused_computation.1.clone.1 | convolution fusion | flops 1610874880 | bytes 4194304 | tf_op jit(solution)/shard_map/while/body/eval_jaxpr/dot_general | solution.py:22
  124.3 1.3 collective-permute-start
  125.6 24.0 %collective-permute-done = f32[512,512]{0,1:T(8,128)S(1)} collective-permute-done((f32[512,512]{0,1:T(8,128)}, f32[512,512]{0,1:T(8,128)S(1)}, u32[]{:S(2)}, u32[]{:S(2)}) %collective-permute-start) | collective-permute-done | bytes 1048608 | tf_op jit(solution)/shard_map/while/body/eval_jaxpr/ppermute | solution.py:12
  149.6 0.0 copy-start.2
  149.6 3.5 %fusion.26 = f32[512,512]{1,0:T(8,128)S(1)} fusion(f32[512,512]{0,1:T(8,128)S(1)} %get-tuple-element.66, f32[512,512]{1,0:T(8,128)S(1)} %get-tuple-element.72), kind=kOutput, calls=%fused_computation.11.clone.1 | convolution fusion | flops 1610612736 | bytes 3145728 | tf_op jit(solution)/shard_map/while/body/eval_jaxpr/dot_general | solution.py:16
  153.1 0.0 copy-done.2
  153.1 4.4 %fusion.27 = f32[512,512]{0,1:T(8,128)} fusion(f32[512,512]{0,1:T(8,128)S(1)} %copy-done.2, f32[512,512]{1,0:T(8,128)S(1)} %fusion.26, f32[512,512]{1,0:T(8,128)S(1)} %get-tuple-element.72), kind=kOutput, calls=%fused_computation.1.clone.1 | convolution fusion | flops 1610874880 | bytes 4194304 | tf_op jit(solution)/shard_map/while/body/eval_jaxpr/dot_general | solution.py:22
  157.5 1.3 collective-permute-start
  158.8 23.2 %collective-permute-done = f32[512,512]{0,1:T(8,128)S(1)} collective-permute-done((f32[512,512]{0,1:T(8,128)}, f32[512,512]{0,1:T(8,128)S(1)}, u32[]{:S(2)}, u32[]{:S(2)}) %collective-permute-start) | collective-permute-done | bytes 1048608 | tf_op jit(solution)/shard_map/while/body/eval_jaxpr/ppermute | solution.py:12
  182.0 0.0 copy-start.2
  182.0 3.5 %fusion.26 = f32[512,512]{1,0:T(8,128)S(1)} fusion(f32[512,512]{0,1:T(8,128)S(1)} %get-tuple-element.66, f32[512,512]{1,0:T(8,128)S(1)} %get-tuple-element.72), kind=kOutput, calls=%fused_computation.11.clone.1 | convolution fusion | flops 1610612736 | bytes 3145728 | tf_op jit(solution)/shard_map/while/body/eval_jaxpr/dot_general | solution.py:16
  185.5 0.0 copy-done.2
  185.5 4.4 %fusion.27 = f32[512,512]{0,1:T(8,128)} fusion(f32[512,512]{0,1:T(8,128)S(1)} %copy-done.2, f32[512,512]{1,0:T(8,128)S(1)} %fusion.26, f32[512,512]{1,0:T(8,128)S(1)} %get-tuple-element.72), kind=kOutput, calls=%fused_computation.1.clone.1 | convolution fusion | flops 1610874880 | bytes 4194304 | tf_op jit(solution)/shard_map/while/body/eval_jaxpr/dot_general | solution.py:22
  190.0 1.3 collective-permute-start
  191.2 22.3 %collective-permute-done = f32[512,512]{0,1:T(8,128)S(1)} collective-permute-done((f32[512,512]{0,1:T(8,128)}, f32[512,512]{0,1:T(8,128)S(1)}, u32[]{:S(2)}, u32[]{:S(2)}) %collective-permute-start) | collective-permute-done | bytes 1048608 | tf_op jit(solution)/shard_map/while/body/eval_jaxpr/ppermute | solution.py:12
  213.6 0.0 copy-start.2
  213.6 3.5 %fusion.26 = f32[512,512]{1,0:T(8,128)S(1)} fusion(f32[512,512]{0,1:T(8,128)S(1)} %get-tuple-element.66, f32[512,512]{1,0:T(8,128)S(1)} %get-tuple-element.72), kind=kOutput, calls=%fused_computation.11.clone.1 | convolution fusion | flops 1610612736 | bytes 3145728 | tf_op jit(solution)/shard_map/while/body/eval_jaxpr/dot_general | solution.py:16
  217.0 0.0 copy-done.2
  217.1 4.4 %fusion.27 = f32[512,512]{0,1:T(8,128)} fusion(f32[512,512]{0,1:T(8,128)S(1)} %copy-done.2, f32[512,512]{1,0:T(8,128)S(1)} %fusion.26, f32[512,512]{1,0:T(8,128)S(1)} %get-tuple-element.72), kind=kOutput, calls=%fused_computation.1.clone.1 | convolution fusion | flops 1610874880 | bytes 4194304 | tf_op jit(solution)/shard_map/while/body/eval_jaxpr/dot_general | solution.py:22
  221.5 1.3 collective-permute-start
  222.8 21.5 %collective-permute-done = f32[512,512]{0,1:T(8,128)S(1)} collective-permute-done((f32[512,512]{0,1:T(8,128)}, f32[512,512]{0,1:T(8,128)S(1)}, u32[]{:S(2)}, u32[]{:S(2)}) %collective-permute-start) | collective-permute-done | bytes 1048608 | tf_op jit(solution)/shard_map/while/body/eval_jaxpr/ppermute | solution.py:12
  244.3 0.0 copy-start.3
  244.3 3.5 %fusion.5 = f32[512,512]{1,0:T(8,128)S(1)} fusion(f32[512,512]{0,1:T(8,128)S(1)} %get-tuple-element.24, f32[1,512,512]{2,1,0:T(8,128)S(1)} %bitcast.41), kind=kOutput, calls=%fused_computation.9 | convolution fusion | flops 1610612736 | bytes 3145728 | tf_op jit(solution)/shard_map/dot_general | solution.py:16
  247.7 0.0 copy-start.4
  247.7 1.0 copy-done.4
  248.7 0.0 copy-done.3
  248.7 3.5 %fusion.3 = f32[512,512]{0,1:T(8,128)S(1)} fusion(f32[512,512]{1,0:T(8,128)S(1)} %fusion.5, f32[1,512,512]{1,2,0:T(8,128)S(1)} %bitcast.44, f32[1,512,512]{2,1,0:T(8,128)S(1)} %bitcast.42), kind=kOutput, calls=%fused_computation.6 | convolution fusion | flops 1610874880 | bytes 4194304 | tf_op jit(solution)/shard_map/dot_general | solution.py:22
  252.2 0.0 copy-done
  252.2 4.1 %fusion.2 = f32[512,512]{1,0:T(8,128)} fusion(f32[512,512]{1,0:T(8,128)} %copy-done.4, f32[512,512]{0,1:T(8,128)S(1)} %fusion.3, f32[512,512]{1,0:T(8,128)S(1)} %copy-done, f32[]{:T(128)S(6)} %select_n.4), kind=kOutput, calls=%fused_computation.4 | convolution fusion | flops 1611137024 | bytes 4194308 | tf_op jit(solution)/shard_map/dot_general | solution.py:22
  256.3 0.0 all-reduce.2.cloned.1.call-update
  256.3 1.3 copy.7
  257.6 78.5 %all-reduce.2.cloned.1.call-done = f32[512,512]{1,0:T(8,128)} async-done(((f32[512,512]{1,0:T(8,128)}), f32[512,512]{1,0:T(8,128)}) %all-reduce.2.cloned.1.call-update) | async-done | bytes 1048592 | tf_op jit(solution)/shard_map/psum | solution.py:50
  336.1 2.3 broadcast_multiply_fusion
Async XLA Ops:
  7.2 245.0 %copy-start = (f32[512,512]{1,0:T(8,128)S(1)}, f32[512,512]{1,0:T(8,128)}, u32[]{:S(2)}) copy-start(f32[512,512]{1,0:T(8,128)} %param.7) | copy-start | bytes 3145732
  7.2 328.9 %all-reduce.2.cloned.1.call-start = ((), (), s32[]{:S(2)}) async-start(), calls=%async_computation | async-start | bytes 2097152 | tf_op jit(solution)/shard_map/psum | solution.py:50
  9.8 1.2 copy-start.1
  11.1 3.5 %copy-start.2 = (f32[512,512]{0,1:T(8,128)S(1)}, f32[512,512]{0,1:T(8,128)}, u32[]{:S(2)}) copy-start(f32[512,512]{0,1:T(8,128)} %get-tuple-element.73) | copy-start | bytes 3145732 | tf_op jit(solution)/shard_map/while
  19.0 28.3 %collective-permute-start = (f32[512,512]{0,1:T(8,128)}, f32[512,512]{0,1:T(8,128)S(1)}, u32[]{:S(2)}, u32[]{:S(2)}) collective-permute-start(f32[512,512]{0,1:T(8,128)} %fusion.27), channel_id=1, source_target_pairs={{4,0},{8,4},{12,8},{16,12},{20,16},{24,20},{28,24},{5,1},{9,5},{13... | collective-permute-start | bytes 3145736 | tf_op jit(solution)/shard_map/while/body/eval_jaxpr/ppermute | solution.py:12
  47.3 3.5 %copy-start.2 = (f32[512,512]{0,1:T(8,128)S(1)}, f32[512,512]{0,1:T(8,128)}, u32[]{:S(2)}) copy-start(f32[512,512]{0,1:T(8,128)} %get-tuple-element.73) | copy-start | bytes 3145732 | tf_op jit(solution)/shard_map/while
  55.2 27.0 %collective-permute-start = (f32[512,512]{0,1:T(8,128)}, f32[512,512]{0,1:T(8,128)S(1)}, u32[]{:S(2)}, u32[]{:S(2)}) collective-permute-start(f32[512,512]{0,1:T(8,128)} %fusion.27), channel_id=1, source_target_pairs={{4,0},{8,4},{12,8},{16,12},{20,16},{24,20},{28,24},{5,1},{9,5},{13... | collective-permute-start | bytes 3145736 | tf_op jit(solution)/shard_map/while/body/eval_jaxpr/ppermute | solution.py:12
  82.2 3.5 %copy-start.2 = (f32[512,512]{0,1:T(8,128)S(1)}, f32[512,512]{0,1:T(8,128)}, u32[]{:S(2)}) copy-start(f32[512,512]{0,1:T(8,128)} %get-tuple-element.73) | copy-start | bytes 3145732 | tf_op jit(solution)/shard_map/while
  90.2 26.2 %collective-permute-start = (f32[512,512]{0,1:T(8,128)}, f32[512,512]{0,1:T(8,128)S(1)}, u32[]{:S(2)}, u32[]{:S(2)}) collective-permute-start(f32[512,512]{0,1:T(8,128)} %fusion.27), channel_id=1, source_target_pairs={{4,0},{8,4},{12,8},{16,12},{20,16},{24,20},{28,24},{5,1},{9,5},{13... | collective-permute-start | bytes 3145736 | tf_op jit(solution)/shard_map/while/body/eval_jaxpr/ppermute | solution.py:12
  116.3 3.5 %copy-start.2 = (f32[512,512]{0,1:T(8,128)S(1)}, f32[512,512]{0,1:T(8,128)}, u32[]{:S(2)}) copy-start(f32[512,512]{0,1:T(8,128)} %get-tuple-element.73) | copy-start | bytes 3145732 | tf_op jit(solution)/shard_map/while
  124.3 25.3 %collective-permute-start = (f32[512,512]{0,1:T(8,128)}, f32[512,512]{0,1:T(8,128)S(1)}, u32[]{:S(2)}, u32[]{:S(2)}) collective-permute-start(f32[512,512]{0,1:T(8,128)} %fusion.27), channel_id=1, source_target_pairs={{4,0},{8,4},{12,8},{16,12},{20,16},{24,20},{28,24},{5,1},{9,5},{13... | collective-permute-start | bytes 3145736 | tf_op jit(solution)/shard_map/while/body/eval_jaxpr/ppermute | solution.py:12
  149.6 3.5 %copy-start.2 = (f32[512,512]{0,1:T(8,128)S(1)}, f32[512,512]{0,1:T(8,128)}, u32[]{:S(2)}) copy-start(f32[512,512]{0,1:T(8,128)} %get-tuple-element.73) | copy-start | bytes 3145732 | tf_op jit(solution)/shard_map/while
  157.5 24.5 %collective-permute-start = (f32[512,512]{0,1:T(8,128)}, f32[512,512]{0,1:T(8,128)S(1)}, u32[]{:S(2)}, u32[]{:S(2)}) collective-permute-start(f32[512,512]{0,1:T(8,128)} %fusion.27), channel_id=1, source_target_pairs={{4,0},{8,4},{12,8},{16,12},{20,16},{24,20},{28,24},{5,1},{9,5},{13... | collective-permute-start | bytes 3145736 | tf_op jit(solution)/shard_map/while/body/eval_jaxpr/ppermute | solution.py:12
  182.0 3.5 %copy-start.2 = (f32[512,512]{0,1:T(8,128)S(1)}, f32[512,512]{0,1:T(8,128)}, u32[]{:S(2)}) copy-start(f32[512,512]{0,1:T(8,128)} %get-tuple-element.73) | copy-start | bytes 3145732 | tf_op jit(solution)/shard_map/while
  190.0 23.6 %collective-permute-start = (f32[512,512]{0,1:T(8,128)}, f32[512,512]{0,1:T(8,128)S(1)}, u32[]{:S(2)}, u32[]{:S(2)}) collective-permute-start(f32[512,512]{0,1:T(8,128)} %fusion.27), channel_id=1, source_target_pairs={{4,0},{8,4},{12,8},{16,12},{20,16},{24,20},{28,24},{5,1},{9,5},{13... | collective-permute-start | bytes 3145736 | tf_op jit(solution)/shard_map/while/body/eval_jaxpr/ppermute | solution.py:12
  213.6 3.5 %copy-start.2 = (f32[512,512]{0,1:T(8,128)S(1)}, f32[512,512]{0,1:T(8,128)}, u32[]{:S(2)}) copy-start(f32[512,512]{0,1:T(8,128)} %get-tuple-element.73) | copy-start | bytes 3145732 | tf_op jit(solution)/shard_map/while
  221.5 22.8 %collective-permute-start = (f32[512,512]{0,1:T(8,128)}, f32[512,512]{0,1:T(8,128)S(1)}, u32[]{:S(2)}, u32[]{:S(2)}) collective-permute-start(f32[512,512]{0,1:T(8,128)} %fusion.27), channel_id=1, source_target_pairs={{4,0},{8,4},{12,8},{16,12},{20,16},{24,20},{28,24},{5,1},{9,5},{13... | collective-permute-start | bytes 3145736 | tf_op jit(solution)/shard_map/while/body/eval_jaxpr/ppermute | solution.py:12
  244.3 4.5 %copy-start.3 = (f32[512,512]{0,1:T(8,128)S(1)}, f32[512,512]{0,1:T(8,128)}, u32[]{:S(2)}) copy-start(f32[512,512]{0,1:T(8,128)} %get-tuple-element.78) | copy-start | bytes 3145732
  247.7 1.0 copy-start.4
Sparse Core Ops, SparseCore 0:
  256.4 79.6 all-reduce.1
where the time goes:
time: 346 us; the launch traced here: 345 us
  waiting for transfers between devices  247 us (71%)
  matrix products  66.4 us (19%)
  between operations  14.1 us (4%)
  starting transfers between devices  9 us (3%)
  local copies, waits for them, and re-layouts  6.14 us (2%)
    ppermute x7, waiting for transfers between devices, passed_along(): return lax.ppermute(block, axis, route)  169 us
    psum x1, waiting for transfers between devices, on_device(): gradient = lax.psum(accumulated, 'tm') / (total_blocks - 1)  78.5 us
    dot_general x9, matrix products, product(): jnp.dot(left, right, precision=highest, preferred_element_type=jnp.float32)  38.7 us
    dot_general x8, matrix products, times_transposed(): lax.dot_general(left, right, (((1,), (1,)), ((), ())), precision=highest,...  27.8 us
    ppermute x7, starting transfers between devices, passed_along(): return lax.ppermute(block, axis, route)  8.96 us
  transfers between devices with their start and end apart: 8, of which 8 were waited for; matrix products, arithmetic and copies ran while one was open for 0% of the time, Pallas kernels for 0%

commit v1 on v0

--- a/solution.py
+++ b/solution.py
@@ -2,6 +2,7 @@
 import jax.numpy as jnp
 from jax import lax
 from jax.sharding import PartitionSpec as P
+from jax.lax import all_gather
 
 highest = lax.Precision.HIGHEST
 
@@ -47,7 +48,12 @@
         jnp.float32
     )
     accumulated = current_entry * (previous_step_cross - product(transition_est, covariance))
-    gradient = lax.psum(accumulated, "tm") / (total_blocks - 1)
+
+    def local_data_view(block_here):
+        shaped = all_gather(block_here, "tm")
+        return jnp.sum(shaped, 0)
+
+    gradient = local_data_view(accumulated) / (total_blocks - 1)
     cov_blocks = jnp.stack(collected[::-1], axis=0)
     return (cov_blocks, gradient)
 

time: 346 us -> 413 us (1.19)
  waiting for transfers between devices: 247 us -> 293 us
  matrix products: 66.4 us -> 86 us
    all_gather x0 -> x1, waiting for transfers between devices: none -> 125 us  [local_data_view(): shaped = all_gather(block_here, 'tm')]
    psum x1 -> x0, waiting for transfers between devices: 78.5 us -> none  [on_device(): gradient = lax.psum(accumulated, 'tm') / (total_blocks - 1)]
    dot_general x9, matrix products: 38.7 us -> 48.5 us  [product(): jnp.dot(left, right, precision=highest, preferred_element_type=jnp.float32)]
    dot_general x8, matrix products: 27.8 us -> 37.6 us  [times_transposed(): lax.dot_general(left, right, (((1,), (1,)), ((), ())), precision=highest,...]
    reduce_sum x0 -> x1, other arithmetic: none -> 4.49 us  [local_data_view(): return jnp.sum(shaped, 0)]
where the time goes in v1:
time: 413 us; the launch traced here: 412 us
  waiting for transfers between devices  293 us (71%)
  matrix products  86 us (21%)
  between operations  14.1 us (3%)
  starting transfers between devices  9 us (2%)
  other arithmetic  5.57 us (1%)
    ppermute x7, waiting for transfers between devices, passed_along(): return lax.ppermute(block, axis, route)  169 us
    all_gather x1, waiting for transfers between devices, local_data_view(): shaped = all_gather(block_here, 'tm')  125 us
    dot_general x9, matrix products, product(): jnp.dot(left, right, precision=highest, preferred_element_type=jnp.float32)  48.5 us
    dot_general x8, matrix products, times_transposed(): lax.dot_general(left, right, (((1,), (1,)), ((), ())), precision=highest,...  37.6 us
    ppermute x7, starting transfers between devices, passed_along(): return lax.ppermute(block, axis, route)  8.96 us
  transfers between devices with their start and end apart: 8, of which 8 were waited for; matrix products, arithmetic and copies ran while one was open for 0% of the time, Pallas kernels for 0%

profile of v1, /device:TPU:0, one launch (start us, length us, event | category | flops | bytes accessed | tf_op | source)
XLA Modules:
  0.0 412.1 jit_solution(4834440265160289454)
XLA Ops:
  7.2 0.0 copy-start
  7.2 0.0 all-gather.3.cloned.1.call-start
  7.2 1.6 copy.5
  8.9 0.1 broadcast_in_dim.3
  9.0 250.2 %while.10 = (s32[]{:T(128)}, f32[512,512]{0,1:T(8,128)S(1)}, f32[512,512]{1,0:T(8,128)}, f32[512,512]{0,1:T(8,128)S(1)}, s32[]{:T(128)}) while((s32[]{:T(128)}, f32[512,512]{0,1:T(8,128)S(1)}, f32[512,512]{1,0:T(8,128)}, f32[512,512]{0,1:T(8,128)S(1)}, s32[]{:T(128)}) %tuple.29), condition=%wide.region_1.0_spmd, body=%wide.region_0.0_spmd.sunk | while | flops 3221487616 | bytes 11534437 | solution.py:42
  9.0 4.7 %fusion.26 = f32[512,512]{1,0:T(8,128)S(1)} fusion(f32[512,512]{0,1:T(8,128)S(1)} %get-tuple-element.66, f32[512,512]{1,0:T(8,128)} %get-tuple-element.72), kind=kOutput, calls=%fused_computation.11.clone.1 | convolution fusion | flops 1610612736 | bytes 3145728 | tf_op jit(solution)/shard_map/while/body/eval_jaxpr/dot_general | solution.py:17
  13.7 5.7 %fusion.27 = f32[512,512]{0,1:T(8,128)} fusion(f32[512,512]{0,1:T(8,128)S(1)} %get-tuple-element.73, f32[512,512]{1,0:T(8,128)S(1)} %fusion.26, f32[512,512]{1,0:T(8,128)} %get-tuple-element.72), kind=kOutput, calls=%fused_computation.1.clone.1 | convolution fusion | flops 1610874880 | bytes 4194304 | tf_op jit(solution)/shard_map/while/body/eval_jaxpr/dot_general | solution.py:23
  19.4 1.3 collective-permute-start
  20.7 27.0 %collective-permute-done = f32[512,512]{0,1:T(8,128)S(1)} collective-permute-done((f32[512,512]{0,1:T(8,128)}, f32[512,512]{0,1:T(8,128)S(1)}, u32[]{:S(2)}, u32[]{:S(2)}) %collective-permute-start) | collective-permute-done | bytes 1048608 | tf_op jit(solution)/shard_map/while/body/eval_jaxpr/ppermute | solution.py:13
  47.6 4.7 %fusion.26 = f32[512,512]{1,0:T(8,128)S(1)} fusion(f32[512,512]{0,1:T(8,128)S(1)} %get-tuple-element.66, f32[512,512]{1,0:T(8,128)} %get-tuple-element.72), kind=kOutput, calls=%fused_computation.11.clone.1 | convolution fusion | flops 1610612736 | bytes 3145728 | tf_op jit(solution)/shard_map/while/body/eval_jaxpr/dot_general | solution.py:17
  52.3 5.7 %fusion.27 = f32[512,512]{0,1:T(8,128)} fusion(f32[512,512]{0,1:T(8,128)S(1)} %get-tuple-element.73, f32[512,512]{1,0:T(8,128)S(1)} %fusion.26, f32[512,512]{1,0:T(8,128)} %get-tuple-element.72), kind=kOutput, calls=%fused_computation.1.clone.1 | convolution fusion | flops 1610874880 | bytes 4194304 | tf_op jit(solution)/shard_map/while/body/eval_jaxpr/dot_general | solution.py:23
  58.0 1.3 collective-permute-start
  59.3 25.7 %collective-permute-done = f32[512,512]{0,1:T(8,128)S(1)} collective-permute-done((f32[512,512]{0,1:T(8,128)}, f32[512,512]{0,1:T(8,128)S(1)}, u32[]{:S(2)}, u32[]{:S(2)}) %collective-permute-start) | collective-permute-done | bytes 1048608 | tf_op jit(solution)/shard_map/while/body/eval_jaxpr/ppermute | solution.py:13
  85.0 4.7 %fusion.26 = f32[512,512]{1,0:T(8,128)S(1)} fusion(f32[512,512]{0,1:T(8,128)S(1)} %get-tuple-element.66, f32[512,512]{1,0:T(8,128)} %get-tuple-element.72), kind=kOutput, calls=%fused_computation.11.clone.1 | convolution fusion | flops 1610612736 | bytes 3145728 | tf_op jit(solution)/shard_map/while/body/eval_jaxpr/dot_general | solution.py:17
  89.8 5.7 %fusion.27 = f32[512,512]{0,1:T(8,128)} fusion(f32[512,512]{0,1:T(8,128)S(1)} %get-tuple-element.73, f32[512,512]{1,0:T(8,128)S(1)} %fusion.26, f32[512,512]{1,0:T(8,128)} %get-tuple-element.72), kind=kOutput, calls=%fused_computation.1.clone.1 | convolution fusion | flops 1610874880 | bytes 4194304 | tf_op jit(solution)/shard_map/while/body/eval_jaxpr/dot_general | solution.py:23
  95.4 1.3 collective-permute-start
  96.7 24.9 %collective-permute-done = f32[512,512]{0,1:T(8,128)S(1)} collective-permute-done((f32[512,512]{0,1:T(8,128)}, f32[512,512]{0,1:T(8,128)S(1)}, u32[]{:S(2)}, u32[]{:S(2)}) %collective-permute-start) | collective-permute-done | bytes 1048608 | tf_op jit(solution)/shard_map/while/body/eval_jaxpr/ppermute | solution.py:13
  121.6 4.7 %fusion.26 = f32[512,512]{1,0:T(8,128)S(1)} fusion(f32[512,512]{0,1:T(8,128)S(1)} %get-tuple-element.66, f32[512,512]{1,0:T(8,128)} %get-tuple-element.72), kind=kOutput, calls=%fused_computation.11.clone.1 | convolution fusion | flops 1610612736 | bytes 3145728 | tf_op jit(solution)/shard_map/while/body/eval_jaxpr/dot_general | solution.py:17
  126.3 5.7 %fusion.27 = f32[512,512]{0,1:T(8,128)} fusion(f32[512,512]{0,1:T(8,128)S(1)} %get-tuple-element.73, f32[512,512]{1,0:T(8,128)S(1)} %fusion.26, f32[512,512]{1,0:T(8,128)} %get-tuple-element.72), kind=kOutput, calls=%fused_computation.1.clone.1 | convolution fusion | flops 1610874880 | bytes 4194304 | tf_op jit(solution)/shard_map/while/body/eval_jaxpr/dot_general | solution.py:23
  132.0 1.3 collective-permute-start
  133.3 24.0 %collective-permute-done = f32[512,512]{0,1:T(8,128)S(1)} collective-permute-done((f32[512,512]{0,1:T(8,128)}, f32[512,512]{0,1:T(8,128)S(1)}, u32[]{:S(2)}, u32[]{:S(2)}) %collective-permute-start) | collective-permute-done | bytes 1048608 | tf_op jit(solution)/shard_map/while/body/eval_jaxpr/ppermute | solution.py:13
  157.3 4.7 %fusion.26 = f32[512,512]{1,0:T(8,128)S(1)} fusion(f32[512,512]{0,1:T(8,128)S(1)} %get-tuple-element.66, f32[512,512]{1,0:T(8,128)} %get-tuple-element.72), kind=kOutput, calls=%fused_computation.11.clone.1 | convolution fusion | flops 1610612736 | bytes 3145728 | tf_op jit(solution)/shard_map/while/body/eval_jaxpr/dot_general | solution.py:17
  162.0 5.7 %fusion.27 = f32[512,512]{0,1:T(8,128)} fusion(f32[512,512]{0,1:T(8,128)S(1)} %get-tuple-element.73, f32[512,512]{1,0:T(8,128)S(1)} %fusion.26, f32[512,512]{1,0:T(8,128)} %get-tuple-element.72), kind=kOutput, calls=%fused_computation.1.clone.1 | convolution fusion | flops 1610874880 | bytes 4194304 | tf_op jit(solution)/shard_map/while/body/eval_jaxpr/dot_general | solution.py:23
  167.7 1.3 collective-permute-start
  169.0 23.2 %collective-permute-done = f32[512,512]{0,1:T(8,128)S(1)} collective-permute-done((f32[512,512]{0,1:T(8,128)}, f32[512,512]{0,1:T(8,128)S(1)}, u32[]{:S(2)}, u32[]{:S(2)}) %collective-permute-start) | collective-permute-done | bytes 1048608 | tf_op jit(solution)/shard_map/while/body/eval_jaxpr/ppermute | solution.py:13
  192.1 4.7 %fusion.26 = f32[512,512]{1,0:T(8,128)S(1)} fusion(f32[512,512]{0,1:T(8,128)S(1)} %get-tuple-element.66, f32[512,512]{1,0:T(8,128)} %get-tuple-element.72), kind=kOutput, calls=%fused_computation.11.clone.1 | convolution fusion | flops 1610612736 | bytes 3145728 | tf_op jit(solution)/shard_map/while/body/eval_jaxpr/dot_general | solution.py:17
  196.8 5.7 %fusion.27 = f32[512,512]{0,1:T(8,128)} fusion(f32[512,512]{0,1:T(8,128)S(1)} %get-tuple-element.73, f32[512,512]{1,0:T(8,128)S(1)} %fusion.26, f32[512,512]{1,0:T(8,128)} %get-tuple-element.72), kind=kOutput, calls=%fused_computation.1.clone.1 | convolution fusion | flops 1610874880 | bytes 4194304 | tf_op jit(solution)/shard_map/while/body/eval_jaxpr/dot_general | solution.py:23
  202.5 1.3 collective-permute-start
  203.8 22.3 %collective-permute-done = f32[512,512]{0,1:T(8,128)S(1)} collective-permute-done((f32[512,512]{0,1:T(8,128)}, f32[512,512]{0,1:T(8,128)S(1)}, u32[]{:S(2)}, u32[]{:S(2)}) %collective-permute-start) | collective-permute-done | bytes 1048608 | tf_op jit(solution)/shard_map/while/body/eval_jaxpr/ppermute | solution.py:13
  226.1 4.7 %fusion.26 = f32[512,512]{1,0:T(8,128)S(1)} fusion(f32[512,512]{0,1:T(8,128)S(1)} %get-tuple-element.66, f32[512,512]{1,0:T(8,128)} %get-tuple-element.72), kind=kOutput, calls=%fused_computation.11.clone.1 | convolution fusion | flops 1610612736 | bytes 3145728 | tf_op jit(solution)/shard_map/while/body/eval_jaxpr/dot_general | solution.py:17
  230.8 5.7 %fusion.27 = f32[512,512]{0,1:T(8,128)} fusion(f32[512,512]{0,1:T(8,128)S(1)} %get-tuple-element.73, f32[512,512]{1,0:T(8,128)S(1)} %fusion.26, f32[512,512]{1,0:T(8,128)} %get-tuple-element.72), kind=kOutput, calls=%fused_computation.1.clone.1 | convolution fusion | flops 1610874880 | bytes 4194304 | tf_op jit(solution)/shard_map/while/body/eval_jaxpr/dot_general | solution.py:23
  236.5 1.3 collective-permute-start
  237.8 21.5 %collective-permute-done = f32[512,512]{0,1:T(8,128)S(1)} collective-permute-done((f32[512,512]{0,1:T(8,128)}, f32[512,512]{0,1:T(8,128)S(1)}, u32[]{:S(2)}, u32[]{:S(2)}) %collective-permute-start) | collective-permute-done | bytes 1048608 | tf_op jit(solution)/shard_map/while/body/eval_jaxpr/ppermute | solution.py:13
  259.2 4.7 %fusion.5 = f32[512,512]{1,0:T(8,128)S(1)} fusion(f32[512,512]{0,1:T(8,128)S(1)} %get-tuple-element.24, f32[1,512,512]{2,1,0:T(8,128)} %bitcast.42), kind=kOutput, calls=%fused_computation.9 | convolution fusion | flops 1610612736 | bytes 3145728 | tf_op jit(solution)/shard_map/dot_general | solution.py:17
  263.9 0.0 copy-start.1
  264.0 1.0 copy-done.1
  264.9 4.7 %fusion.3 = f32[512,512]{0,1:T(8,128)S(1)} fusion(f32[512,512]{1,0:T(8,128)S(1)} %fusion.5, f32[1,512,512]{1,2,0:T(8,128)S(1)} %bitcast.45, f32[1,512,512]{2,1,0:T(8,128)} %bitcast.43), kind=kOutput, calls=%fused_computation.6 | convolution fusion | flops 1610874880 | bytes 4194304 | tf_op jit(solution)/shard_map/dot_general | solution.py:23
  269.6 0.0 copy-done
  269.6 4.1 fusion.2
  273.7 0.0 all-gather.3.cloned.1.call-update
  273.7 1.3 copy.7
  275.0 124.7 %all-gather.3.cloned.1.call-done = f32[4096,512]{1,0:T(8,128)} async-done(((f32[512,512]{1,0:T(8,128)}), f32[4096,512]{1,0:T(8,128)}) %all-gather.3.cloned.1.call-update) | async-done | bytes 8388624 | tf_op jit(solution)/shard_map/all_gather | solution.py:53
  399.7 4.5 %reduce_sum.9 = f32[512,512]{1,0:T(8,128)S(1)} reduce(f32[8,512,512]{2,1,0:T(8,128)} %bitcast.47, f32[]{:T(128)} %constant.6.clone.1), dimensions={0}, to_apply=%region_2.3 | reduce | flops 1835008 | bytes 9437188 | tf_op jit(solution)/shard_map/reduce_sum | solution.py:54
  404.2 1.1 broadcast_multiply_fusion
Async XLA Ops:
  7.2 262.5 %copy-start = (f32[512,512]{1,0:T(8,128)S(1)}, f32[512,512]{1,0:T(8,128)}, u32[]{:S(2)}) copy-start(f32[512,512]{1,0:T(8,128)} %param.7) | copy-start | bytes 3145732
  7.2 392.5 %all-gather.3.cloned.1.call-start = ((), (), s32[]{:S(2)}) async-start(), calls=%async_computation | async-start | bytes 9437184 | tf_op jit(solution)/shard_map/all_gather | solution.py:53
  19.4 28.3 %collective-permute-start = (f32[512,512]{0,1:T(8,128)}, f32[512,512]{0,1:T(8,128)S(1)}, u32[]{:S(2)}, u32[]{:S(2)}) collective-permute-start(f32[512,512]{0,1:T(8,128)} %fusion.27), channel_id=1, source_target_pairs={{4,0},{8,4},{12,8},{16,12},{20,16},{24,20},{28,24},{5,1},{9,5},{13... | collective-permute-start | bytes 3145736 | tf_op jit(solution)/shard_map/while/body/eval_jaxpr/ppermute | solution.py:13
  58.0 27.0 %collective-permute-start = (f32[512,512]{0,1:T(8,128)}, f32[512,512]{0,1:T(8,128)S(1)}, u32[]{:S(2)}, u32[]{:S(2)}) collective-permute-start(f32[512,512]{0,1:T(8,128)} %fusion.27), channel_id=1, source_target_pairs={{4,0},{8,4},{12,8},{16,12},{20,16},{24,20},{28,24},{5,1},{9,5},{13... | collective-permute-start | bytes 3145736 | tf_op jit(solution)/shard_map/while/body/eval_jaxpr/ppermute | solution.py:13
  95.4 26.2 %collective-permute-start = (f32[512,512]{0,1:T(8,128)}, f32[512,512]{0,1:T(8,128)S(1)}, u32[]{:S(2)}, u32[]{:S(2)}) collective-permute-start(f32[512,512]{0,1:T(8,128)} %fusion.27), channel_id=1, source_target_pairs={{4,0},{8,4},{12,8},{16,12},{20,16},{24,20},{28,24},{5,1},{9,5},{13... | collective-permute-start | bytes 3145736 | tf_op jit(solution)/shard_map/while/body/eval_jaxpr/ppermute | solution.py:13
  132.0 25.3 %collective-permute-start = (f32[512,512]{0,1:T(8,128)}, f32[512,512]{0,1:T(8,128)S(1)}, u32[]{:S(2)}, u32[]{:S(2)}) collective-permute-start(f32[512,512]{0,1:T(8,128)} %fusion.27), channel_id=1, source_target_pairs={{4,0},{8,4},{12,8},{16,12},{20,16},{24,20},{28,24},{5,1},{9,5},{13... | collective-permute-start | bytes 3145736 | tf_op jit(solution)/shard_map/while/body/eval_jaxpr/ppermute | solution.py:13
  167.7 24.5 %collective-permute-start = (f32[512,512]{0,1:T(8,128)}, f32[512,512]{0,1:T(8,128)S(1)}, u32[]{:S(2)}, u32[]{:S(2)}) collective-permute-start(f32[512,512]{0,1:T(8,128)} %fusion.27), channel_id=1, source_target_pairs={{4,0},{8,4},{12,8},{16,12},{20,16},{24,20},{28,24},{5,1},{9,5},{13... | collective-permute-start | bytes 3145736 | tf_op jit(solution)/shard_map/while/body/eval_jaxpr/ppermute | solution.py:13
  202.5 23.6 %collective-permute-start = (f32[512,512]{0,1:T(8,128)}, f32[512,512]{0,1:T(8,128)S(1)}, u32[]{:S(2)}, u32[]{:S(2)}) collective-permute-start(f32[512,512]{0,1:T(8,128)} %fusion.27), channel_id=1, source_target_pairs={{4,0},{8,4},{12,8},{16,12},{20,16},{24,20},{28,24},{5,1},{9,5},{13... | collective-permute-start | bytes 3145736 | tf_op jit(solution)/shard_map/while/body/eval_jaxpr/ppermute | solution.py:13
  236.5 22.7 %collective-permute-start = (f32[512,512]{0,1:T(8,128)}, f32[512,512]{0,1:T(8,128)S(1)}, u32[]{:S(2)}, u32[]{:S(2)}) collective-permute-start(f32[512,512]{0,1:T(8,128)} %fusion.27), channel_id=1, source_target_pairs={{4,0},{8,4},{12,8},{16,12},{20,16},{24,20},{28,24},{5,1},{9,5},{13... | collective-permute-start | bytes 3145736 | tf_op jit(solution)/shard_map/while/body/eval_jaxpr/ppermute | solution.py:13
  263.9 1.0 copy-start.1
Sparse Core Ops, SparseCore 0:
  273.8 125.8 all-gather.2
